TPU v7x, 256 devices: a whole 4x4x8 slice. The times are simulated.
256 devices in a mesh: facet: 16 (over y, x_hi, core), bl: 16 (over z, x_lo).
Axes of the slice: x: 4 (x_hi: 2, x_lo: 2; x = x_hi * 2 + x_lo), y: 4, z: 8, core: 2. Of those that a mesh axis runs over, the one named last changes fastest.
Arguments:
- facet_model: bfloat16 [16, 1024, 1024], P('facet', 'bl'), may hold values from -0.005859375 to 0.005859375
- screens: bfloat16 [16, 256, 64, 128], P('facet', 'bl'), may hold values from 0.099609375 to 1.8984375
- observed: float32 [192, 64, 128], P('bl'), may hold values from -24 to 24
- offsets: int32 [192, 2], P('bl'), may hold values from 0 to 4032
- stations: int32 [192, 2], P('bl'), may hold values from 0 to 255
- counts: int32 [16], P('bl'), may hold values from 1 to 12, as said below
Outputs:
- residual_vis: float32 [192, 64, 128], P('bl')
- residual_image: float32 [16, 1024, 1024], P('facet', 'bl')
Inputs may be any that keep to these rules, and one draw needn't show every extreme that they name: `counts`: some baseline block has all 12 slots live.
All inputs are finite; a program needn't handle non-finite values.
Results may differ from a plain program's by a relative error of at most 0.0061.
Values may be sent and summed in bfloat16 or wider, within the bound.
No kernel may reach another device: no remote copies, remote signals or barrier semaphores. Data moves between devices by JAX's collectives and lax.ppermute only.
A program may use at most 64 MiB of HBM per device.

v0:
```python
import math
import jax
import jax.numpy as jnp
from jax import lax
from jax.sharding import PartitionSpec as P

FGRID = 4


def tables(offset_u, offset_v, facet_id, tile_width, facet_cells):
    grid_cells = FGRID * facet_cells
    corner_x = facet_id // FGRID * facet_cells
    corner_y = facet_id % FGRID * facet_cells
    pixel_index = jnp.arange(facet_cells, dtype=jnp.int32)
    cell_index = jnp.arange(tile_width, dtype=jnp.int32)
    phase_u = jnp.mod(
        (offset_u + cell_index)[:, None] * (corner_x + pixel_index)[None, :], grid_cells
    )
    phase_v = jnp.mod(
        (offset_v + cell_index)[:, None] * (corner_y + pixel_index)[None, :], grid_cells
    )
    angle_u = phase_u.astype(jnp.float32) * (2.0 * math.pi / grid_cells)
    angle_v = phase_v.astype(jnp.float32) * (2.0 * math.pi / grid_cells)
    tab_u = jnp.concatenate([jnp.cos(angle_u), -jnp.sin(angle_u)], axis=0).astype(jnp.bfloat16)
    table_vertical = jnp.concatenate([jnp.cos(angle_v), jnp.sin(angle_v)], axis=0).astype(
        jnp.bfloat16
    )
    return (tab_u, table_vertical)


def half_splits(value):
    half_width = value.shape[-1] // 2
    return (value[..., :half_width], value[..., half_width:])


def complex_times(left_re, left_im, right_re, right_im):
    return (left_re * right_re - left_im * right_im, left_re * right_im + left_im * right_re)


def times_conj(left_re, left_im, right_re, right_im):
    return (left_re * right_re + left_im * right_im, left_im * right_re - left_re * right_im)


def per_device(facet_model, screens, observed, offsets, stations, counts):
    tile_count = observed.shape[0]
    tile_width = observed.shape[1]
    facet_cells = facet_model.shape[2]
    bl_devices = lax.axis_size("bl")
    facet_id = lax.axis_index("facet")
    make_tables = jax.vmap(tables, in_axes=(0, 0, None, None, None))
    tab_u, table_vertical = make_tables(
        offsets[:, 0], offsets[:, 1], facet_id, tile_width, facet_cells
    )
    upper_portion = jnp.einsum(
        "tkn,np->tkp",
        tab_u,
        lax.all_gather(facet_model[0], "bl", axis=0, tiled=True),
        preferred_element_type=jnp.float32,
    ).astype(jnp.bfloat16)
    block_groups = jnp.einsum(
        "gsf,gmf->gsm", upper_portion, table_vertical, preferred_element_type=jnp.float32
    )
    real_part = (
        block_groups[:, :tile_width, :tile_width] + block_groups[:, tile_width:, tile_width:]
    )
    imag_part = (
        block_groups[:, tile_width:, :tile_width] - block_groups[:, :tile_width, tile_width:]
    )
    all_screens = lax.all_gather(screens[0], "bl", axis=0, tiled=True)
    first_station_gain = jnp.take(all_screens, stations[:, 0], axis=0).astype(jnp.float32)
    gain_q = jnp.take(all_screens, stations[:, 1], axis=0).astype(jnp.float32)
    p_re, p_im = half_splits(first_station_gain)
    q_re, q_im = half_splits(gain_q)
    y_re, y_im = complex_times(p_re, p_im, real_part, imag_part)
    x_re, x_im = times_conj(y_re, y_im, q_re, q_im)
    contribution = jnp.concatenate([x_re, x_im], axis=2)
    live_mask = (jnp.arange(tile_count, dtype=jnp.int32) < counts[0])[:, None, None]
    predicted = lax.psum(contribution, "facet")
    residual = jnp.where(live_mask, observed - predicted, jnp.zeros_like(observed))
    r_re, r_im = half_splits(residual)
    z_re, z_im = times_conj(r_re, r_im, p_re, p_im)
    w_re, w_im = complex_times(z_re, z_im, q_re, q_im)
    w_re = w_re.astype(jnp.bfloat16)
    w_im = w_im.astype(jnp.bfloat16)
    stacked = jnp.concatenate(
        [jnp.concatenate([w_re, -w_im], axis=2), jnp.concatenate([w_im, w_re], axis=2)], axis=1
    )
    q_two = jnp.einsum(
        "tuk,tky->tuy", stacked, table_vertical, preferred_element_type=jnp.float32
    ).astype(jnp.bfloat16)
    image_scale = 1.0 / (32.0 * tile_width * math.sqrt(tile_count * bl_devices))
    row_count = facet_cells // bl_devices
    whole_image = jnp.einsum("tkx,tky->xy", tab_u, q_two, preferred_element_type=jnp.float32)
    summed = lax.psum(whole_image, "bl")
    own_rows = lax.dynamic_slice_in_dim(summed, lax.axis_index("bl") * row_count, row_count, 0)
    residual_image = (own_rows * image_scale)[None]
    return (residual, residual_image)


def solution(mesh):
    in_specs = (
        P("facet", "bl", None),
        P("facet", "bl", None, None),
        P("bl", None, None),
        P("bl", None),
        P("bl", None),
        P("bl"),
    )
    out_specs = (P("bl", None, None), P("facet", "bl", None))
    return jax.shard_map(
        per_device, mesh=mesh, in_specs=in_specs, out_specs=out_specs, check_vma=False
    )
```

profile of v0, /device:TPU:16, one launch (start us, length us, event | category | flops | bytes accessed | tf_op | source)
XLA Modules:
  0.0 557.0 jit_solution(6302353294279317188)
XLA Ops:
  7.2 0.0 all-gather.7.cloned.1.call-start
  7.2 0.7 all-gather.7.cloned.1.call-update
  7.9 0.0 all-gather.5.cloned.1.call-start
  7.9 0.7 all-gather.5.cloned.1.call-update
  8.6 0.0 all-reduce.3.cloned.1.call-start
  8.7 0.8 compare_and_fusion.1
  9.5 0.8 slice_bitcast_fusion.1
  10.3 0.1 iota_add_fusion
  10.4 14.1 %cosine_convert_fusion = (bf16[12,64,1024]{2,1,0:T(8,128)(2,1)S(1)}, bf16[12,64,1024]{2,1,0:T(8,128)(2,1)}) fusion(s32[1024]{0:T(1024)S(1)} %iota_add_fusion.2, s32[12,64]{1,0:T(8,128)S(1)} %get-tuple-element.24), kind=kLoop, calls=%fused_computation.23 | loop fusion | flops 12582912 | bytes 3152896 | tf_op jit(solution)/shard_map/convert
  24.4 14.2 %cosine_convert_fusion.1 = (bf16[12,64,1024]{2,1,0:T(8,128)(2,1)}, bf16[12,64,1024]{2,1,0:T(8,128)(2,1)}) fusion(s32[1024]{0:T(1024)S(1)} %iota_add_fusion.3, s32[12,64]{1,0:T(8,128)S(1)} %get-tuple-element.25), kind=kLoop, calls=%fused_computation.27 | loop fusion | flops 13369344 | bytes 3152896 | tf_op jit(solution)/shard_map/convert.2
  38.7 46.7 %all-gather.7.cloned.1.call-done = bf16[1,1024,1024]{2,1,0:T(8,128)(2,1)} async-done(((bf16[1,64,1024]{2,1,0:T(8,128)(2,1)}), bf16[1,1024,1024]{2,1,0:T(8,128)(2,1)}) %all-gather.7.cloned.1.call-update) | async-done | bytes 2097168 | tf_op jit(solution)/shard_map/all_gather | solution.py:57
  85.4 7.2 %fusion.8 = f32[12,128,128]{2,1,0:T(8,128)S(1)} fusion(bf16[12,64,1024]{2,1,0:T(8,128)(2,1)} %get-tuple-element.17, bf16[12,64,1024]{2,1,0:T(8,128)(2,1)S(1)} %get-tuple-element.16, bf16[1,1024,1024]{2,1,0:T(8,128)(2,1)} %all-gather.7.cloned.1.call-done, bf16[12,64,1024]{2,1,0:T(8,128)(2,1)} %get-tuple-element.15, bf16[12,64,1024]{2,1,0:T(8,128)(2,1)} %get-tuple-element.14), kind=kOutput, calls=%fused_computation.24 | convolution fusion | flops 3638034432 | bytes 9175040 | tf_op jit(solution)/shard_map/gsf,gmf->gsm/dot_general | solution.py:60
  92.6 92.0 %all-gather.5.cloned.1.call-done = bf16[1,256,64,128]{3,2,0,1:T(8,128)(2,1)} async-done(((bf16[1,16,64,128]{3,2,0,1:T(8,128)(2,1)}), bf16[1,256,64,128]{3,2,0,1:T(8,128)(2,1)}) %all-gather.5.cloned.1.call-update) | async-done | bytes 4194320 | tf_op jit(solution)/shard_map/all_gather | solution.py:69
  184.6 2.8 gather_fusion.1
  187.4 2.8 gather_fusion
  190.1 0.1 select_convert_fusion
  190.3 0.0 copy-start.1
  190.3 0.5 multiply_add_fusion.1
  190.8 0.2 multiply_subtract_fusion.1
  191.0 0.9 pad_maximum_fusion.11
  191.9 0.0 all-reduce.3.cloned.1.call-update
  191.9 0.2 all-reduce.5.cloned.1.call-start
  192.8 134.5 %all-reduce.3.cloned.1.call-done = f32[12,64,128]{2,1,0:T(8,128)} async-done(((f32[12,64,128]{2,1,0:T(8,128)}), f32[12,64,128]{2,1,0:T(8,128)}) %all-reduce.3.cloned.1.call-update) | async-done | bytes 393232 | tf_op jit(solution)/shard_map/psum | solution.py:78
  327.3 0.0 copy-done.1
  327.3 1.1 subtract_select_fusion
  328.4 0.0 copy-start
  328.4 0.4 fusion.39
  328.8 0.2 subtract_convert_fusion
  329.0 8.6 %fusion.12 = f32[1024,1024]{1,0:T(8,128)} fusion(bf16[12,64,1024]{2,1,0:T(8,128)(2,1)} %get-tuple-element.17, bf16[12,64,1024]{2,1,0:T(8,128)(2,1)S(1)} %get-tuple-element.16, bf16[12,64,1024]{2,1,0:T(8,128)(2,1)} %get-tuple-element.15, bf16[12,64,1024]{2,1,0:T(8,128)(2,1)} %get-tuple-element.14, bf16[12,64,64]{2,1,0:T(8,128)(2,1)S(1)} %subtract_convert_fusion, ...), kind=kOutput, calls=%fused_computation.29 | convolution fusion | flops 3639607296 | bytes 10780672 | tf_op jit(solution)/shard_map/tkx,tky->xy/dot_general | solution.py:93
  337.6 0.0 all-reduce.5.cloned.1.call-update
  337.7 211.1 %all-reduce.5.cloned.1.call-done = f32[1024,1024]{1,0:T(8,128)} async-done(((f32[1024,1024]{1,0:T(8,128)}), f32[1024,1024]{1,0:T(8,128)}) %all-reduce.5.cloned.1.call-update) | async-done | bytes 4194320 | tf_op jit(solution)/shard_map/psum | solution.py:94
  548.8 1.7 multiply_bitcast_fusion
  (6 shorter events, 0.0 us)
Async XLA Ops:
  7.2 78.2 %all-gather.7.cloned.1.call-start = ((), (), s32[]{:S(2)}) async-start(), calls=%async_computation.3 | async-start | bytes 2228224 | tf_op jit(solution)/shard_map/all_gather | solution.py:57
  7.9 176.7 %all-gather.5.cloned.1.call-start = ((), (), s32[]{:S(2)}) async-start(), calls=%async_computation.2 | async-start | bytes 4456448 | tf_op jit(solution)/shard_map/all_gather | solution.py:69
  8.6 318.6 %all-reduce.3.cloned.1.call-start = ((), (), s32[]{:S(2)}) async-start(), calls=%async_computation | async-start | bytes 786432 | tf_op jit(solution)/shard_map/psum | solution.py:78
  190.3 137.0 %copy-start.1 = (f32[12,64,128]{2,1,0:T(8,128)S(1)}, f32[12,64,128]{2,1,0:T(8,128)}, u32[]{:S(2)}) copy-start(f32[12,64,128]{2,1,0:T(8,128)} %param.10) | copy-start | bytes 1179652
  191.9 356.9 %all-reduce.5.cloned.1.call-start = ((), (), s32[]{:S(2)}) async-start(), calls=%async_computation.1 | async-start | bytes 8388608 | tf_op jit(solution)/shard_map/psum | solution.py:94
  328.4 9.2 %copy-start = (f32[12,64,128]{2,1,0:T(8,128)}, f32[12,64,128]{2,1,0:T(8,128)S(1)}, u32[]{:S(2)}) copy-start(f32[12,64,128]{2,1,0:T(8,128)S(1)} %subtract_select_fusion) | copy-start | bytes 1179652
Sparse Core Ops, SparseCore 0:
  9.8 75.5 all-gather.6
  87.2 97.3 all-gather.4
  192.0 135.2 all-reduce.2
  337.8 210.9 all-reduce.4
where the time goes:
time: 557 us
  waiting for transfers between devices  486 us (87%)
  other arithmetic  34.2 us (6%)
  matrix products  15.9 us (3%)
  between operations  14.6 us (3%)
  local copies, waits for them, and re-layouts  6.31 us (1%)
    psum x1, waiting for transfers between devices, per_device(): summed = lax.psum(whole_image, 'bl')  211 us
    psum x1, waiting for transfers between devices, per_device(): predicted = lax.psum(contribution, 'facet')  134 us
    all_gather x1, waiting for transfers between devices, per_device(): all_screens = lax.all_gather(screens[0], 'bl', axis=0, tiled=True)  92 us
    all_gather x1, waiting for transfers between devices, per_device(): lax.all_gather(facet_model[0], 'bl', axis=0, tiled=True)  46.7 us
    another operation x2, other arithmetic  28.3 us
  transfers between devices with their start and end apart: 4, of which 4 were waited for; matrix products, arithmetic and copies ran while one was open for 7% of the time, Pallas kernels for 0%

commit v1 on v0

--- a/solution.py
+++ b/solution.py
@@ -51,10 +51,19 @@
     tab_u, table_vertical = make_tables(
         offsets[:, 0], offsets[:, 1], facet_id, tile_width, facet_cells
     )
+    map_strings_by_axis = lambda local, mesh_dim, axis_k: jnp.concatenate(
+        lax.all_to_all(
+            jnp.stack([local] * lax.axis_size(mesh_dim)),
+            axis_name=mesh_dim,
+            split_axis=0,
+            concat_axis=0,
+        ),
+        axis=axis_k,
+    )
     upper_portion = jnp.einsum(
         "tkn,np->tkp",
         tab_u,
-        lax.all_gather(facet_model[0], "bl", axis=0, tiled=True),
+        map_strings_by_axis(facet_model[0], "bl", 0),
         preferred_element_type=jnp.float32,
     ).astype(jnp.bfloat16)
     block_groups = jnp.einsum(

time: 557 us -> 515 us (0.925)
  waiting for transfers between devices: 486 us -> 431 us
  starting transfers between devices: 0.34 us -> 9.8 us
    all_gather x1 -> x0, waiting for transfers between devices: 46.7 us -> none  [per_device(): lax.all_gather(facet_model[0], 'bl', axis=0, tiled=True)]
    all_gather x1, waiting for transfers between devices: 92 us -> 54.8 us  [per_device(): all_screens = lax.all_gather(screens[0], 'bl', axis=0, tiled=True)]
    all_to_all x0 -> x1, waiting for transfers between devices: none -> 31.5 us  [per_device(): lax.all_to_all(jnp.stack([local] * lax.axis_size(mesh_dim)), axis_name=me...]
    all_to_all x0 -> x1, starting transfers between devices: none -> 9.5 us  [per_device(): lax.all_to_all(jnp.stack([local] * lax.axis_size(mesh_dim)), axis_name=me...]
  transfers between devices with their start and end apart: 4 -> 4, of which waited for: 4 -> 4; matrix products, arithmetic and copies ran while one was open for 7% -> 8% of each run, Pallas kernels for 0% -> 0%
where the time goes in v1:
time: 515 us
  waiting for transfers between devices  431 us (84%)
  other arithmetic  33.6 us (7%)
  matrix products  16.3 us (3%)
  between operations  14.6 us (3%)
  starting transfers between devices  9.8 us (2%)
  local copies, waits for them, and re-layouts  9.47 us (2%)
    psum x1, waiting for transfers between devices, per_device(): summed = lax.psum(whole_image, 'bl')  211 us
    psum x1, waiting for transfers between devices, per_device(): predicted = lax.psum(contribution, 'facet')  133 us
    all_gather x1, waiting for transfers between devices, per_device(): all_screens = lax.all_gather(screens[0], 'bl', axis=0, tiled=True)  54.8 us
    all_to_all x1, waiting for transfers between devices, per_device(): lax.all_to_all(jnp.stack([local] * lax.axis_size(mesh_dim)), axis_name=me...  31.5 us
    another operation x2, other arithmetic  28.4 us
  transfers between devices with their start and end apart: 4, of which 4 were waited for; matrix products, arithmetic and copies ran while one was open for 8% of the time, Pallas kernels for 0%

profile of v1, /device:TPU:16, one launch (start us, length us, event | category | flops | bytes accessed | tf_op | source)
XLA Modules:
  0.0 515.0 jit_solution(2448831931276313944)
XLA Ops:
  7.2 0.0 all-gather.3.cloned.1.call-start
  7.2 0.7 all-gather.3.cloned.1.call-update
  7.9 2.5 stack.3
  10.5 9.5 %all-to-all-start = ((bf16[16,64,1024]{2,1,0:T(8,128)(2,1)}), bf16[16,64,1024]{2,1,0:T(8,128)(2,1)S(1)}, u32[]{:S(2)}, u32[]{:S(2)}) async-start(bf16[16,64,1024]{2,1,0:T(8,128)(2,1)} %stack.3), calls=%async_computation | async-start | bytes 4194304 | tf_op jit(solution)/shard_map/all_to_all | solution.py:55
  20.0 0.0 all-reduce.3.cloned.1.call-start
  20.1 0.1 iota_add_fusion
  20.2 14.1 %cosine_convert_fusion = (bf16[12,64,1024]{2,1,0:T(8,128)(2,1)}, bf16[12,64,1024]{2,1,0:T(8,128)(2,1)}) fusion(s32[1024]{0:T(1024)S(1)} %iota_add_fusion.2, s32[12,64]{1,0:T(8,128)S(1)} %get-tuple-element.24), kind=kLoop, calls=%fused_computation.23 | loop fusion | flops 12582912 | bytes 3152896 | tf_op jit(solution)/shard_map/convert
  34.3 14.2 %cosine_convert_fusion.1 = (bf16[12,64,1024]{2,1,0:T(8,128)(2,1)}, bf16[12,64,1024]{2,1,0:T(8,128)(2,1)}) fusion(s32[1024]{0:T(1024)S(1)} %iota_add_fusion.3, s32[12,64]{1,0:T(8,128)S(1)} %get-tuple-element.25), kind=kLoop, calls=%fused_computation.27 | loop fusion | flops 13369344 | bytes 3152896 | tf_op jit(solution)/shard_map/convert.2
  48.5 31.5 %all-to-all-done = bf16[16,64,1024]{2,1,0:T(8,128)(2,1)S(1)} async-done(((bf16[16,64,1024]{2,1,0:T(8,128)(2,1)}), bf16[16,64,1024]{2,1,0:T(8,128)(2,1)S(1)}, u32[]{:S(2)}, u32[]{:S(2)}) %all-to-all-start) | async-done | bytes 2097184 | tf_op jit(solution)/shard_map/all_to_all | solution.py:55
  80.0 1.4 copy-done.1
  81.4 7.7 %fusion.8 = f32[12,128,128]{2,1,0:T(8,128)S(1)} fusion(bf16[12,64,1024]{2,1,0:T(8,128)(2,1)} %get-tuple-element.17, bf16[12,64,1024]{2,1,0:T(8,128)(2,1)} %get-tuple-element.16, bf16[1024,1024,1]{1,0,2:T(8,128)(2,1)} %bitcast.23, bf16[12,64,1024]{2,1,0:T(8,128)(2,1)} %get-tuple-element.15, bf16[12,64,1024]{2,1,0:T(8,128)(2,1)} %get-tuple-element.14), kind=kOutput, calls=%fused_computation.24 | convolution fusion | flops 3638034432 | bytes 9175040 | tf_op jit(solution)/shard_map/gsf,gmf->gsm/dot_general | solution.py:69
  89.1 54.8 %all-gather.3.cloned.1.call-done = bf16[1,256,64,128]{3,2,0,1:T(8,128)(2,1)} async-done(((bf16[1,16,64,128]{3,2,0,1:T(8,128)(2,1)}), bf16[1,256,64,128]{3,2,0,1:T(8,128)(2,1)}) %all-gather.3.cloned.1.call-update) | async-done | bytes 4194320 | tf_op jit(solution)/shard_map/all_gather | solution.py:78
  143.9 2.8 gather_fusion.1
  146.6 2.8 gather_fusion
  149.4 0.1 select_convert_fusion
  149.5 0.1 select_convert_fusion.1
  149.6 0.0 copy-start.3
  149.7 0.5 multiply_add_fusion.1
  150.1 0.2 multiply_subtract_fusion.1
  150.3 0.9 pad_maximum_fusion.11
  151.2 0.0 all-reduce.3.cloned.1.call-update
  151.3 0.2 all-reduce.5.cloned.1.call-start
  152.2 0.0 copy-start.2
  152.2 133.3 %all-reduce.3.cloned.1.call-done = f32[12,64,128]{2,1,0:T(8,128)} async-done(((f32[12,64,128]{2,1,0:T(8,128)}), f32[12,64,128]{2,1,0:T(8,128)}) %all-reduce.3.cloned.1.call-update) | async-done | bytes 393232 | tf_op jit(solution)/shard_map/psum | solution.py:87
  285.4 1.1 subtract_select_fusion
  286.6 0.0 copy-start
  286.6 0.4 fusion.34
  286.9 0.2 subtract_convert_fusion
  287.2 8.6 %fusion.12 = f32[1024,1024]{1,0:T(8,128)} fusion(bf16[12,64,1024]{2,1,0:T(8,128)(2,1)} %get-tuple-element.17, bf16[12,64,1024]{2,1,0:T(8,128)(2,1)S(1)} %copy-done.2, bf16[12,64,1024]{2,1,0:T(8,128)(2,1)} %get-tuple-element.15, bf16[12,64,1024]{2,1,0:T(8,128)(2,1)} %get-tuple-element.14, bf16[12,64,64]{2,1,0:T(8,128)(2,1)S(1)} %subtract_convert_fusion, ...), kind=kOutput, calls=%fused_computation.29 | convolution fusion | flops 3639607296 | bytes 10780672 | tf_op jit(solution)/shard_map/tkx,tky->xy/dot_general | solution.py:102
  295.8 0.0 all-reduce.5.cloned.1.call-update
  295.8 211.0 %all-reduce.5.cloned.1.call-done = f32[1024,1024]{1,0:T(8,128)} async-done(((f32[1024,1024]{1,0:T(8,128)}), f32[1024,1024]{1,0:T(8,128)}) %all-reduce.5.cloned.1.call-update) | async-done | bytes 4194320 | tf_op jit(solution)/shard_map/psum | solution.py:103
  506.8 1.7 multiply_bitcast_fusion
  (14 shorter events, 0.1 us)
Async XLA Ops:
  7.2 136.7 %all-gather.3.cloned.1.call-start = ((), (), s32[]{:S(2)}) async-start(), calls=%async_computation.3 | async-start | bytes 4456448 | tf_op jit(solution)/shard_map/all_gather | solution.py:78
  7.9 12.2 %copy-start.4 = (s32[12,2]{0,1:T(2,128)S(1)}, s32[12,2]{0,1:T(2,128)}, u32[]{:S(2)}) copy-start(s32[12,2]{0,1:T(2,128)} %param.12) | copy-start | bytes 292
  7.9 12.2 %copy-start.5 = (s32[12,2]{0,1:T(2,128)S(1)}, s32[12,2]{0,1:T(2,128)}, u32[]{:S(2)}) copy-start(s32[12,2]{0,1:T(2,128)} %param.11) | copy-start | bytes 292
  10.5 69.5 %all-to-all-start = ((bf16[16,64,1024]{2,1,0:T(8,128)(2,1)}), bf16[16,64,1024]{2,1,0:T(8,128)(2,1)S(1)}, u32[]{:S(2)}, u32[]{:S(2)}) async-start(bf16[16,64,1024]{2,1,0:T(8,128)(2,1)} %stack.3), calls=%async_computation | async-start | bytes 4194304 | tf_op jit(solution)/shard_map/all_to_all | solution.py:55
  20.0 265.5 %all-reduce.3.cloned.1.call-start = ((), (), s32[]{:S(2)}) async-start(), calls=%async_computation.1 | async-start | bytes 786432 | tf_op jit(solution)/shard_map/psum | solution.py:87
  80.0 1.4 copy-start.1
  149.6 135.8 %copy-start.3 = (f32[12,64,128]{2,1,0:T(8,128)S(1)}, f32[12,64,128]{2,1,0:T(8,128)}, u32[]{:S(2)}) copy-start(f32[12,64,128]{2,1,0:T(8,128)} %param.10) | copy-start | bytes 1179652
  151.3 355.6 %all-reduce.5.cloned.1.call-start = ((), (), s32[]{:S(2)}) async-start(), calls=%async_computation.2 | async-start | bytes 8388608 | tf_op jit(solution)/shard_map/psum | solution.py:103
  152.2 135.0 %copy-start.2 = (bf16[12,64,1024]{2,1,0:T(8,128)(2,1)S(1)}, bf16[12,64,1024]{2,1,0:T(8,128)(2,1)}, u32[]{:S(2)}) copy-start(bf16[12,64,1024]{2,1,0:T(8,128)(2,1)} %get-tuple-element.16) | copy-start | bytes 4718596
  286.6 9.2 %copy-start = (f32[12,64,128]{2,1,0:T(8,128)}, f32[12,64,128]{2,1,0:T(8,128)S(1)}, u32[]{:S(2)}) copy-start(f32[12,64,128]{2,1,0:T(8,128)S(1)} %subtract_select_fusion) | copy-start | bytes 1179652
Sparse Core Ops, SparseCore 0:
  9.8 134.0 all-gather.2
  151.4 134.0 all-reduce.2
  295.9 210.8 all-reduce.4
